TPU v7x, 256 devices: a whole 4x4x8 slice. The times are simulated.
256 devices in a mesh: blk: 32 (over x_lo, z, core), head: 8 (over y, x_hi).
Axes of the slice: x: 4 (x_hi: 2, x_lo: 2; x = x_hi * 2 + x_lo), y: 4, z: 8, core: 2. Of those that a mesh axis runs over, the one named last changes fastest.
Arguments:
- queries: bfloat16 [2, 4096, 32, 128], P(None, 'blk', 'head'), may hold values from -30 to 30
- new_keys: bfloat16 [2, 4096, 16, 128], P(None, 'blk', 'head'), may hold values from -30 to 30
- new_values: bfloat16 [2, 4096, 16, 128], P(None, 'blk', 'head'), may hold values from -6 to 6
- pool_keys: bfloat16 [64, 128, 16, 128], P('blk', None, 'head'), may hold values from -30 to 30
- pool_values: bfloat16 [64, 128, 16, 128], P('blk', None, 'head'), may hold values from -6 to 6
- page_table: int32 [2, 32], replicated, may hold values from 0 to 63, as said below
- cache_len: int32 [2], replicated, may hold values from 1024 to 4096, as said below
- out_weight: bfloat16 [32, 128, 4608], P('head'), may hold values from -0.09375 to 0.09375
- residual: bfloat16 [2, 4096, 4608], P(None, ('blk', 'head')), may hold values from -6 to 6
- post_gain: float32 [4608], replicated, may hold values from 0.1 to 1.9
Outputs:
- mixed: bfloat16 [2, 4096, 4608], P(None, ('blk', 'head'))
Inputs may be any that keep to these rules, and one draw needn't show every extreme that they name: `page_table`: every pool page appears exactly once in the table. `cache_len`: one request has exactly 4096 cached tokens.
All inputs are finite; a program needn't handle non-finite values.
Results may differ from a plain program's by a relative error of at most 0.015.
Values may be sent and summed in bfloat16 or wider, within the bound.
A program may use at most 128 MiB of HBM per device.

v0:
```python
import jax
import jax.numpy as jnp
from jax import lax
from jax.sharding import PartitionSpec as P

soft_cap = 50.0
score_scale = 144.0 ** (-0.5)
norm_eps = 1e-06


def group_pages(page_count, page_len):
    width = max(1, min(page_count, 2048 // page_len))
    while page_count % width:
        width -= 1
    return width


def attend_pages(running, grouped, key_pages, value_pages, valid_keys):
    page_count, page_len, kv_heads, head_dim = key_pages.shape
    tok_rows = valid_keys.shape[1]
    width = group_pages(page_count, page_len)
    groups = page_count // width
    key_groups = key_pages.reshape(groups, width * page_len, kv_heads, head_dim)
    value_groups = value_pages.reshape(groups, width * page_len, kv_heads, head_dim)
    valid_groups = (
        valid_keys.reshape(groups, width, tok_rows, page_len)
        .transpose(0, 2, 1, 3)
        .reshape(groups, tok_rows, width * page_len)
    )

    def compute(carry_in, key_block, value_block, valid_block):
        numerator, denominator = carry_in
        scores = (
            jnp.einsum("tkgd,skd->kgts", grouped, key_block, preferred_element_type=jnp.float32)
            * score_scale
        )
        capped = soft_cap * jnp.tanh(scores / soft_cap)
        weights = jnp.where(valid_block[None, None], jnp.exp(capped), 0.0).astype(jnp.bfloat16)
        numerator = numerator + jnp.einsum(
            "kgts,skd->tkgd", weights, value_block, preferred_element_type=jnp.float32
        )
        denominator = denominator + jnp.sum(weights.astype(jnp.float32), axis=-1)
        return (numerator, denominator)

    def one_group(carry_in, inputs):
        key_block, value_block, valid_block = inputs
        carry_out = compute(carry_in, key_block, value_block, valid_block)
        return (carry_out, None)

    result, _ = lax.scan(one_group, running, (key_groups, value_groups, valid_groups))
    return result


def shards(
    queries,
    new_keys,
    new_values,
    pool_keys,
    pool_values,
    page_table,
    cache_len,
    out_weight,
    residual,
    post_gain,
):
    req_count, per_req, heads_here, head_dim = queries.shape
    tok_dev = req_count * per_req
    kv_here = new_keys.shape[2]
    page_len = pool_keys.shape[1]
    slot_count = page_table.shape[1]
    blk_place = lax.axis_index("blk")
    row_ids = jnp.arange(tok_dev, dtype=jnp.int32)
    row_request = row_ids // per_req
    row_offset = blk_place * per_req + row_ids % per_req
    grouped = queries.reshape(tok_dev, kv_here, heads_here // kv_here, head_dim)
    page_rows = jnp.arange(page_len, dtype=jnp.int32)
    request_ids = jnp.arange(req_count, dtype=jnp.int32)
    row_onehot = row_request[:, None] == request_ids[None, :]
    start_carry = (
        jnp.zeros((tok_dev, kv_here, heads_here // kv_here, head_dim), jnp.float32),
        jnp.zeros((kv_here, heads_here // kv_here, tok_dev), jnp.float32),
    )
    pieces = (
        lax.all_gather(pool_keys, "blk", axis=0, tiled=True),
        lax.all_gather(pool_values, "blk", axis=0, tiled=True),
    )
    page_ids = jnp.arange(pieces[0].shape[0], dtype=jnp.int32)
    matches = page_ids[:, None, None] == page_table[None, :, :]
    slot_index = jnp.sum(
        jnp.where(matches, jnp.arange(slot_count, dtype=jnp.int32)[None, None, :], 0), axis=2
    )
    owned_page = jnp.any(matches, axis=2)
    position = slot_index[:, :, None] * page_len + page_rows[None, None, :]
    keep_keys = owned_page[:, :, None] & (position < cache_len[None, :, None])
    running = attend_pages(
        start_carry,
        grouped,
        pieces[0],
        pieces[1],
        jnp.any(keep_keys[:, None, :, :] & row_onehot[None, :, :, None], axis=2),
    )
    pieces = (
        lax.all_gather(new_keys, "blk", axis=1, tiled=True),
        lax.all_gather(new_values, "blk", axis=1, tiled=True),
    )
    piece_pages = pieces[0].shape[1] // page_len
    page_index = jnp.arange(req_count * piece_pages, dtype=jnp.int32)
    firsts = page_index % piece_pages * page_len
    key_pages = pieces[0].reshape(req_count * piece_pages, page_len, kv_here, head_dim)
    value_pages = pieces[1].reshape(req_count * piece_pages, page_len, kv_here, head_dim)
    offsets = firsts[:, None] + page_rows[None, :]
    same_request = (page_index // piece_pages)[:, None] == row_request[None, :]
    running = attend_pages(
        running,
        grouped,
        key_pages,
        value_pages,
        same_request[:, :, None] & (offsets[:, None, :] <= row_offset[None, :, None]),
    )
    numerator, denominator = running
    attended = (numerator / jnp.transpose(denominator, (2, 0, 1))[..., None]).astype(jnp.bfloat16)
    head_count = lax.axis_size("head")
    share = per_req // head_count
    feature_len = heads_here * head_dim
    attended = (
        attended.reshape(req_count, head_count, share, feature_len)
        .transpose(1, 0, 2, 3)
        .reshape(tok_dev, feature_len)
    )
    weight_rows = out_weight.reshape(feature_len, out_weight.shape[2])
    projected = lax.psum_scatter(
        jnp.dot(attended, weight_rows, preferred_element_type=jnp.float32).astype(jnp.bfloat16),
        "head",
        scatter_dimension=0,
        tiled=True,
    ).astype(jnp.float32)
    projected = projected.reshape(req_count, share, projected.shape[1])
    inv_rms = lax.rsqrt(jnp.mean(projected * projected, axis=-1, keepdims=True) + norm_eps)
    mixed_out = residual.astype(jnp.float32) + post_gain * projected * inv_rms
    return mixed_out.astype(jnp.bfloat16)


def solution(mesh):
    placed = (
        P(None, "blk", "head", None),
        P(None, "blk", "head", None),
        P(None, "blk", "head", None),
        P("blk", None, "head", None),
        P("blk", None, "head", None),
        P(),
        P(),
        P("head", None, None),
        P(None, ("blk", "head"), None),
        P(),
    )
    return jax.shard_map(
        shards,
        mesh=mesh,
        in_specs=placed,
        out_specs=P(None, ("blk", "head"), None),
        check_vma=False,
    )
```

profile of v0, /device:TPU:32, one launch (start us, length us, event | category | flops | bytes accessed | tf_op | source)
XLA Modules:
  0.0 406.5 jit_solution(9550354351666353231)
XLA Ops:
  6.5 0.0 all-gather.7.cloned.1.call-start
  6.5 1.6 copy.33
  8.1 0.0 all-gather.7.cloned.1.call-update
  8.2 0.0 all-gather.5.cloned.1.call-start
  8.2 1.6 copy.29
  9.8 0.0 all-gather.5.cloned.1.call-update
  9.8 0.0 all-gather.9.cloned.1.call-start
  9.9 1.6 copy.37
  11.5 0.0 all-gather.9.cloned.1.call-update
  11.5 0.0 all-gather.11.cloned.1.call-start
  11.5 1.6 copy.38
  13.1 0.0 all-gather.11.cloned.1.call-update
  13.1 0.0 reduce-scatter.2.cloned.1.call-start
  13.2 0.8 select_reduce_fusion
  14.0 0.1 copy.31
  14.1 0.8 fusion.16
  14.9 0.1 copy.30
  15.0 0.9 compare_and_fusion
  15.9 3.5 and_reduce_fusion
  19.4 4.8 %copy.32 = pred[4,256,16,128]{1,3,2,0:T(8,128)(4,1)} copy(pred[4,256,16,128]{3,1,2,0:T(8,128)(4,1)S(1)} %bitcast.108) | data formatting | bytes 4194304 | tf_op jit(solution)/shard_map/transpose | solution.py:27
  24.3 0.1 broadcast_compare_fusion
  24.4 0.1 broadcast_bitcast_fusion
  24.5 1.7 bitcast_and_fusion
  26.2 51.5 %all-gather.7.cloned.1.call-done = bf16[64,128,2,128]{3,1,0,2:T(8,128)(2,1)} async-done(((bf16[2,128,2,128]{3,1,0,2:T(8,128)(2,1)}), bf16[64,128,2,128]{3,1,0,2:T(8,128)(2,1)}) %all-gather.7.cloned.1.call-update) | async-done | bytes 4194320 | tf_op jit(solution)/shard_map/all_gather | solution.py:84
  77.7 68.5 %all-gather.5.cloned.1.call-done = bf16[64,128,2,128]{3,1,0,2:T(8,128)(2,1)} async-done(((bf16[2,128,2,128]{3,1,0,2:T(8,128)(2,1)}), bf16[64,128,2,128]{3,1,0,2:T(8,128)(2,1)}) %all-gather.5.cloned.1.call-update) | async-done | bytes 4194320 | tf_op jit(solution)/shard_map/all_gather | solution.py:85
  146.3 41.6 %while.30 = (s32[]{:T(128)}, f32[256,2,2,128]{0,3,2,1:T(8,128)S(1)}, f32[2,2,256]{2,1,0:T(2,128)S(1)}, bf16[4,2048,2,128]{3,1,0,2:T(8,128)(2,1)}, pred[4,256,204...) while((s32[]{:T(128)}, ...), condition=%wide.region_5.6_spmd.clone, body=%wide.region_3.5_spmd.clone.sunk | while | flops 1086587904 | bytes 13386860 | solution.py:50
  146.3 1.2 dynamic-slice_bitcast_fusion.5
  147.5 5.7 %convert_reduce_fusion.5 = (f32[2,2,256]{2,1,0:T(2,128)S(1)}, bf16[2,2,256,2048]{2,3,1,0:T(8,128)(2,1)}) fusion(bf16[256,2,2,128]{3,0,2,1:T(8,128)(2,1)S(1)} %get-tuple-element.391, bf16[4,2048,2,128]{3,1,0,2:T(8,128)(2,1)} %get-tuple-element.390, s32[]{:T(128)} %get-tuple-element.376, pred[256,2048]{0,1:T(8,128)(4,1)S(1)} %dynamic-slice_bitcast_fusion.5), kind=kOutput, calls=%fused_computation.14.clone.1 | convolution fusion | flops 549452800 | bytes 6033920 | tf_op jit(solution)/shard_map/while/body/eval_jaxpr/tkgd,skd->kgts/dot_general | solution.py:34
  153.2 3.4 fusion.47
  156.6 1.2 dynamic-slice_bitcast_fusion.5
  157.9 5.7 %convert_reduce_fusion.5 = (f32[2,2,256]{2,1,0:T(2,128)S(1)}, bf16[2,2,256,2048]{2,3,1,0:T(8,128)(2,1)}) fusion(bf16[256,2,2,128]{3,0,2,1:T(8,128)(2,1)S(1)} %get-tuple-element.391, bf16[4,2048,2,128]{3,1,0,2:T(8,128)(2,1)} %get-tuple-element.390, s32[]{:T(128)} %get-tuple-element.376, pred[256,2048]{0,1:T(8,128)(4,1)S(1)} %dynamic-slice_bitcast_fusion.5), kind=kOutput, calls=%fused_computation.14.clone.1 | convolution fusion | flops 549452800 | bytes 6033920 | tf_op jit(solution)/shard_map/while/body/eval_jaxpr/tkgd,skd->kgts/dot_general | solution.py:34
  163.5 3.5 fusion.47
  167.0 1.2 dynamic-slice_bitcast_fusion.5
  168.3 5.7 %convert_reduce_fusion.5 = (f32[2,2,256]{2,1,0:T(2,128)S(1)}, bf16[2,2,256,2048]{2,3,1,0:T(8,128)(2,1)}) fusion(bf16[256,2,2,128]{3,0,2,1:T(8,128)(2,1)S(1)} %get-tuple-element.391, bf16[4,2048,2,128]{3,1,0,2:T(8,128)(2,1)} %get-tuple-element.390, s32[]{:T(128)} %get-tuple-element.376, pred[256,2048]{0,1:T(8,128)(4,1)S(1)} %dynamic-slice_bitcast_fusion.5), kind=kOutput, calls=%fused_computation.14.clone.1 | convolution fusion | flops 549452800 | bytes 6033920 | tf_op jit(solution)/shard_map/while/body/eval_jaxpr/tkgd,skd->kgts/dot_general | solution.py:34
  173.9 3.5 fusion.47
  177.5 1.2 dynamic-slice_bitcast_fusion.5
  178.7 5.7 %convert_reduce_fusion.5 = (f32[2,2,256]{2,1,0:T(2,128)S(1)}, bf16[2,2,256,2048]{2,3,1,0:T(8,128)(2,1)}) fusion(bf16[256,2,2,128]{3,0,2,1:T(8,128)(2,1)S(1)} %get-tuple-element.391, bf16[4,2048,2,128]{3,1,0,2:T(8,128)(2,1)} %get-tuple-element.390, s32[]{:T(128)} %get-tuple-element.376, pred[256,2048]{0,1:T(8,128)(4,1)S(1)} %dynamic-slice_bitcast_fusion.5), kind=kOutput, calls=%fused_computation.14.clone.1 | convolution fusion | flops 549452800 | bytes 6033920 | tf_op jit(solution)/shard_map/while/body/eval_jaxpr/tkgd,skd->kgts/dot_general | solution.py:34
  184.4 3.5 fusion.47
  187.9 26.7 %all-gather.9.cloned.1.call-done = bf16[2,4096,2,128]{3,1,0,2:T(8,128)(2,1)} async-done(((bf16[2,128,2,128]{3,1,0,2:T(8,128)(2,1)}), bf16[2,4096,2,128]{3,1,0,2:T(8,128)(2,1)}) %all-gather.9.cloned.1.call-update) | async-done | bytes 4194320 | tf_op jit(solution)/shard_map/all_gather | solution.py:104
  214.6 68.1 %all-gather.11.cloned.1.call-done = bf16[2,4096,2,128]{3,1,0,2:T(8,128)(2,1)} async-done(((bf16[2,128,2,128]{3,1,0,2:T(8,128)(2,1)}), bf16[2,4096,2,128]{3,1,0,2:T(8,128)(2,1)}) %all-gather.11.cloned.1.call-update) | async-done | bytes 4194320 | tf_op jit(solution)/shard_map/all_gather | solution.py:103
  282.7 26.7 %while.29 = (s32[]{:T(128)}, f32[256,2,2,128]{0,3,2,1:T(8,128)S(1)}, f32[2,2,256]{2,1,0:T(2,128)S(1)}, bf16[4,2048,2,128]{3,1,0,2:T(8,128)(2,1)}, pred[4,256,204...) while((s32[]{:T(128)}, ...), condition=%wide.region_8.9_spmd, body=%wide.region_6.8_spmd.sunk | while | flops 1086455808 | bytes 13386841 | solution.py:50
  282.7 0.2 dynamic-slice_bitcast_fusion.4
  282.9 4.3 %convert_reduce_fusion.4 = (f32[2,2,256]{2,1,0:T(2,128)S(1)}, bf16[2,2,256,2048]{2,3,1,0:T(8,128)(2,1)S(1)}) fusion(bf16[256,2,2,128]{3,0,2,1:T(8,128)(2,1)S(1)} %get-tuple-element.416, bf16[4,2048,2,128]{3,1,0,2:T(8,128)(2,1)} %get-tuple-element.415, s32[]{:T(128)} %get-tuple-element.402, pred[256,2048]{0,1:T(8,128)(4,1)S(1)} %dynamic-slice_bitcast_fusion.4), kind=kOutput, calls=%fused_computation.2.clone.1 | convolution fusion | flops 549452800 | bytes 6033920 | tf_op jit(solution)/shard_map/while/body/eval_jaxpr/tkgd,skd->kgts/dot_general | solution.py:34
  287.2 2.1 fusion.43
  289.4 0.2 dynamic-slice_bitcast_fusion.4
  289.5 4.3 %convert_reduce_fusion.4 = (f32[2,2,256]{2,1,0:T(2,128)S(1)}, bf16[2,2,256,2048]{2,3,1,0:T(8,128)(2,1)S(1)}) fusion(bf16[256,2,2,128]{3,0,2,1:T(8,128)(2,1)S(1)} %get-tuple-element.416, bf16[4,2048,2,128]{3,1,0,2:T(8,128)(2,1)} %get-tuple-element.415, s32[]{:T(128)} %get-tuple-element.402, pred[256,2048]{0,1:T(8,128)(4,1)S(1)} %dynamic-slice_bitcast_fusion.4), kind=kOutput, calls=%fused_computation.2.clone.1 | convolution fusion | flops 549452800 | bytes 6033920 | tf_op jit(solution)/shard_map/while/body/eval_jaxpr/tkgd,skd->kgts/dot_general | solution.py:34
  293.9 2.1 fusion.43
  296.0 0.2 dynamic-slice_bitcast_fusion.4
  296.2 4.3 %convert_reduce_fusion.4 = (f32[2,2,256]{2,1,0:T(2,128)S(1)}, bf16[2,2,256,2048]{2,3,1,0:T(8,128)(2,1)S(1)}) fusion(bf16[256,2,2,128]{3,0,2,1:T(8,128)(2,1)S(1)} %get-tuple-element.416, bf16[4,2048,2,128]{3,1,0,2:T(8,128)(2,1)} %get-tuple-element.415, s32[]{:T(128)} %get-tuple-element.402, pred[256,2048]{0,1:T(8,128)(4,1)S(1)} %dynamic-slice_bitcast_fusion.4), kind=kOutput, calls=%fused_computation.2.clone.1 | convolution fusion | flops 549452800 | bytes 6033920 | tf_op jit(solution)/shard_map/while/body/eval_jaxpr/tkgd,skd->kgts/dot_general | solution.py:34
  300.5 2.1 fusion.43
  302.7 0.2 dynamic-slice_bitcast_fusion.4
  302.9 4.3 %convert_reduce_fusion.4 = (f32[2,2,256]{2,1,0:T(2,128)S(1)}, bf16[2,2,256,2048]{2,3,1,0:T(8,128)(2,1)S(1)}) fusion(bf16[256,2,2,128]{3,0,2,1:T(8,128)(2,1)S(1)} %get-tuple-element.416, bf16[4,2048,2,128]{3,1,0,2:T(8,128)(2,1)} %get-tuple-element.415, s32[]{:T(128)} %get-tuple-element.402, pred[256,2048]{0,1:T(8,128)(4,1)S(1)} %dynamic-slice_bitcast_fusion.4), kind=kOutput, calls=%fused_computation.2.clone.1 | convolution fusion | flops 549452800 | bytes 6033920 | tf_op jit(solution)/shard_map/while/body/eval_jaxpr/tkgd,skd->kgts/dot_general | solution.py:34
  307.2 2.1 fusion.43
  309.5 0.2 copy.41
  309.6 0.1 reshape.208
  309.8 0.0 copy-start
  309.8 0.0 copy-start.2
  309.8 5.2 %convolution_convert_fusion = bf16[256,4608]{1,0:T(8,128)(2,1)} fusion(bf16[256,512]{1,0:T(8,128)(2,1)S(1)} %bitcast.115, bf16[512,4608]{1,0:T(8,128)(2,1)} %bitcast.116), kind=kOutput, calls=%fused_computation.27 | convolution fusion | flops 1209139200 | bytes 7340032 | tf_op jit(solution)/shard_map/dot_general | solution.py:132
  315.0 0.0 reduce-scatter.2.cloned.1.call-update
  315.0 81.9 %reduce-scatter.2.cloned.1.call-done = bf16[32,4608]{1,0:T(8,128)(2,1)} async-done(((bf16[256,4608]{1,0:T(8,128)(2,1)}), bf16[32,4608]{1,0:T(8,128)(2,1)}) %reduce-scatter.2.cloned.1.call-update) | async-done | bytes 294928 | tf_op jit(solution)/shard_map/reduce_scatter | solution.py:131
  396.9 1.1 multiply_reduce_fusion
  398.0 0.1 rsqrt.12
  398.1 0.0 copy-done
  398.1 1.8 add_convert_fusion
  (25 shorter events, 0.3 us)
Async XLA Ops:
  6.5 17.7 %copy-start.1 = (bf16[2,128,4,128]{3,2,1,0:T(4,128)(2,1)S(1)}, bf16[2,128,4,128]{3,2,1,0:T(4,128)(2,1)}, u32[]{:S(2)}) copy-start(bf16[2,128,4,128]{3,2,1,0:T(4,128)(2,1)} %param.14) | copy-start | bytes 786436
  6.5 71.2 %all-gather.7.cloned.1.call-start = ((), (), s32[]{:S(2)}) async-start(), calls=%async_computation.2 | async-start | bytes 4325376 | tf_op jit(solution)/shard_map/all_gather | solution.py:84
  8.2 138.1 %all-gather.5.cloned.1.call-start = ((), (), s32[]{:S(2)}) async-start(), calls=%async_computation.1 | async-start | bytes 4325376 | tf_op jit(solution)/shard_map/all_gather | solution.py:85
  9.8 204.8 %all-gather.9.cloned.1.call-start = ((), (), s32[]{:S(2)}) async-start(), calls=%async_computation.3 | async-start | bytes 4325376 | tf_op jit(solution)/shard_map/all_gather | solution.py:104
  11.5 271.2 %all-gather.11.cloned.1.call-start = ((), (), s32[]{:S(2)}) async-start(), calls=%async_computation.4 | async-start | bytes 4325376 | tf_op jit(solution)/shard_map/all_gather | solution.py:103
  13.1 383.8 %reduce-scatter.2.cloned.1.call-start = ((), (), s32[]{:S(2)}) async-start(), calls=%async_computation.5 | async-start | bytes 2654208 | tf_op jit(solution)/shard_map/reduce_scatter | solution.py:131
  309.8 88.4 %copy-start = (bf16[2,16,4608]{2,1,0:T(8,128)(2,1)S(1)}, bf16[2,16,4608]{2,1,0:T(8,128)(2,1)}, u32[]{:S(2)}) copy-start(bf16[2,16,4608]{2,1,0:T(8,128)(2,1)} %param.22) | copy-start | bytes 884740
  309.8 88.3 %copy-start.2 = (f32[4608]{0:T(1024)S(1)}, f32[4608]{0:T(1024)}, u32[]{:S(2)}) copy-start(f32[4608]{0:T(1024)} %param.23) | copy-start | bytes 55300
Sparse Core Ops, SparseCore 0:
  9.2 68.4 all-gather.6
  79.6 66.6 all-gather.4
  148.2 66.3 all-gather.8
  216.3 66.3 all-gather.10
  315.1 81.7 reduce-scatter.1
where the time goes:
time: 407 us; the launch traced here: 406 us
  waiting for transfers between devices  297 us (73%)
  matrix products  67.5 us (17%)
  local copies, waits for them, and re-layouts  17.6 us (4%)
  between operations  13.3 us (3%)
  other arithmetic  10.9 us (3%)
    reduce_scatter x1, waiting for transfers between devices, shards(): lax.psum_scatter(jnp.dot(attended, weight_rows, preferred_element_type=jn...  81.9 us
    all_gather x1, waiting for transfers between devices, shards(): lax.all_gather(pool_values, 'blk', axis=0, tiled=True)  68.5 us
    all_gather x1, waiting for transfers between devices, shards(): lax.all_gather(new_keys, 'blk', axis=1, tiled=True)  68.1 us
    all_gather x1, waiting for transfers between devices, shards(): lax.all_gather(pool_keys, 'blk', axis=0, tiled=True)  51.5 us
    dot_general x8, matrix products, compute(): jnp.einsum('tkgd,skd->kgts', grouped, key_block, preferred_element_type=j...  39.8 us
    all_gather x1, waiting for transfers between devices, shards(): lax.all_gather(new_values, 'blk', axis=1, tiled=True)  26.7 us
    dot_general x8, matrix products, compute(): jnp.einsum('kgts,skd->tkgd', weights, value_block, preferred_element_type...  22.4 us
  transfers between devices with their start and end apart: 5, of which 5 were waited for; matrix products, arithmetic and copies ran while one was open for 15% of the time, Pallas kernels for 0%

commit v1 on v0

--- a/solution.py
+++ b/solution.py
@@ -6,6 +6,11 @@
 soft_cap = 50.0
 score_scale = 144.0 ** (-0.5)
 norm_eps = 1e-06
+
+
+def exchange_gather(x, axis, dim):
+    outgoing = jnp.stack([x] * lax.axis_size(axis))
+    return jnp.concatenate(lax.all_to_all(outgoing, axis, 0, 0), axis=dim)
 
 
 def group_pages(page_count, page_len):
@@ -101,7 +106,7 @@
     )
     pieces = (
         lax.all_gather(new_keys, "blk", axis=1, tiled=True),
-        lax.all_gather(new_values, "blk", axis=1, tiled=True),
+        exchange_gather(new_values, "blk", 1),
     )
     piece_pages = pieces[0].shape[1] // page_len
     page_index = jnp.arange(req_count * piece_pages, dtype=jnp.int32)

time: 407 us -> 386 us (0.948)
  waiting for transfers between devices: 297 us -> 261 us
  starting transfers between devices: 0.17 us -> 9.97 us
  local copies, waits for them, and re-layouts: 17.6 us -> 23.7 us
    all_to_all x0 -> x1, waiting for transfers between devices: none -> 100 us  [exchange_gather(): return jnp.concatenate(lax.all_to_all(outgoing, axis, 0, 0), axis=dim)]
    all_gather x1, waiting for transfers between devices: 51.5 us -> 0.01 us  [shards(): lax.all_gather(pool_keys, 'blk', axis=0, tiled=True)]
    all_gather x1, waiting for transfers between devices: 68.1 us -> 26.7 us  [shards(): lax.all_gather(new_keys, 'blk', axis=1, tiled=True)]
    all_gather x1 -> x0, waiting for transfers between devices: 26.7 us -> none  [shards(): lax.all_gather(new_values, 'blk', axis=1, tiled=True)]
    all_gather x1, waiting for transfers between devices: 68.5 us -> 52.2 us  [shards(): lax.all_gather(pool_values, 'blk', axis=0, tiled=True)]
    all_to_all x0 -> x1, starting transfers between devices: none -> 9.85 us  [exchange_gather(): return jnp.concatenate(lax.all_to_all(outgoing, axis, 0, 0), axis=dim)]
    all_to_all x0 -> x1, local copies, waits for them, and re-layouts: none -> 4.74 us  [exchange_gather(): return jnp.concatenate(lax.all_to_all(outgoing, axis, 0, 0), axis=dim)]
  transfers between devices with their start and end apart: 5 -> 5, of which waited for: 5 -> 4; matrix products, arithmetic and copies ran while one was open for 15% -> 16% of each run, Pallas kernels for 0% -> 0%
where the time goes in v1:
time: 386 us; the launch traced here: 385 us
  waiting for transfers between devices  261 us (68%)
  matrix products  67.6 us (18%)
  local copies, waits for them, and re-layouts  23.7 us (6%)
  between operations  13.3 us (3%)
  starting transfers between devices  9.97 us (3%)
  other arithmetic  8.87 us (2%)
    all_to_all x1, waiting for transfers between devices, exchange_gather(): return jnp.concatenate(lax.all_to_all(outgoing, axis, 0, 0), axis=dim)  100 us
    reduce_scatter x1, waiting for transfers between devices, shards(): lax.psum_scatter(jnp.dot(attended, weight_rows, preferred_element_type=jn...  81.8 us
    all_gather x1, waiting for transfers between devices, shards(): lax.all_gather(pool_values, 'blk', axis=0, tiled=True)  52.2 us
    dot_general x8, matrix products, compute(): jnp.einsum('tkgd,skd->kgts', grouped, key_block, preferred_element_type=j...  39.9 us
    all_gather x1, waiting for transfers between devices, shards(): lax.all_gather(new_keys, 'blk', axis=1, tiled=True)  26.7 us
    dot_general x8, matrix products, compute(): jnp.einsum('kgts,skd->tkgd', weights, value_block, preferred_element_type...  22.4 us
    all_to_all x1, starting transfers between devices, exchange_gather(): return jnp.concatenate(lax.all_to_all(outgoing, axis, 0, 0), axis=dim)  9.85 us
  transfers between devices with their start and end apart: 5, of which 4 were waited for; matrix products, arithmetic and copies ran while one was open for 16% of the time, Pallas kernels for 0%

profile of v1, /device:TPU:32, one launch (start us, length us, event | category | flops | bytes accessed | tf_op | source)
XLA Modules:
  0.0 384.5 jit_solution(17649202417222002196)
XLA Ops:
  6.5 1.6 copy.47
  8.1 0.0 all-gather.6.cloned.1.call-update
  8.1 0.0 all-gather.4.cloned.1.call-start
  8.2 1.6 copy.43
  9.8 0.0 all-gather.4.cloned.1.call-update
  9.8 0.9 copy.51
  10.7 3.0 stack.2
  13.7 9.8 %all-to-all-start = ((bf16[32,2,128,2,128]{4,2,1,3,0:T(8,128)(2,1)}), bf16[32,2,128,2,128]{4,2,1,3,0:T(8,128)(2,1)}, u32[]{:S(2)}, u32[]{:S(2)}) async-start(bf16[32,2,128,2,128]{4,2,1,3,0:T(8,128)(2,1)} %stack.2), calls=%async_computation | async-start | bytes 8388608 | tf_op jit(solution)/shard_map/all_to_all | solution.py:13
  23.6 0.0 copy-start.1
  23.6 0.0 all-gather.8.cloned.1.call-start
  23.6 0.0 copy-done.2
  23.7 0.7 copy.53
  24.3 0.0 all-gather.8.cloned.1.call-update
  24.3 0.0 reduce-scatter.2.cloned.1.call-start
  24.4 0.1 select_reduce_fusion
  24.5 0.1 copy.45
  24.6 0.1 fusion.16
  24.7 0.1 copy.44
  24.9 0.2 compare_and_fusion
  25.1 3.5 and_reduce_fusion
  28.6 4.8 %copy.46 = pred[4,256,16,128]{1,3,2,0:T(8,128)(4,1)} copy(pred[4,256,16,128]{3,1,2,0:T(8,128)(4,1)S(1)} %bitcast.111) | data formatting | bytes 4194304 | tf_op jit(solution)/shard_map/transpose | solution.py:32
  33.5 0.1 broadcast_compare_fusion
  33.6 0.1 broadcast_bitcast_fusion
  33.7 1.7 bitcast_and_fusion
  35.4 100.0 %all-to-all-done = bf16[32,2,128,2,128]{4,2,1,3,0:T(8,128)(2,1)} async-done(((bf16[32,2,128,2,128]{4,2,1,3,0:T(8,128)(2,1)}), bf16[32,2,128,2,128]{4,2,1,3,0:T(8,128)(2,1)}, u32[]{:S(2)}, u32[]{:S(2)}) %all-to-all-start) | async-done | bytes 4194336 | tf_op jit(solution)/shard_map/all_to_all | solution.py:13
  135.5 4.7 %copy.52 = bf16[32,2,128,2,128]{4,2,0,1,3:T(8,128)(2,1)} copy(bf16[32,2,128,2,128]{4,2,1,3,0:T(8,128)(2,1)} %all-to-all-done) | data formatting | bytes 8388608 | tf_op jit(solution)/shard_map/all_to_all | solution.py:13
  140.2 52.2 %all-gather.4.cloned.1.call-done = bf16[64,128,2,128]{3,1,0,2:T(8,128)(2,1)} async-done(((bf16[2,128,2,128]{3,1,0,2:T(8,128)(2,1)}), bf16[64,128,2,128]{3,1,0,2:T(8,128)(2,1)}) %all-gather.4.cloned.1.call-update) | async-done | bytes 4194320 | tf_op jit(solution)/shard_map/all_gather | solution.py:90
  192.5 41.6 %while.30 = (s32[]{:T(128)}, f32[256,2,2,128]{0,3,2,1:T(8,128)S(1)}, f32[2,2,256]{2,1,0:T(2,128)S(1)}, bf16[4,2048,2,128]{3,1,0,2:T(8,128)(2,1)}, pred[4,256,204...) while((s32[]{:T(128)}, ...), condition=%wide.region_5.6_spmd.clone, body=%wide.region_3.5_spmd.clone.sunk | while | flops 1086587904 | bytes 13386860 | solution.py:55
  192.5 1.2 dynamic-slice_bitcast_fusion.5
  193.7 5.7 %convert_reduce_fusion.5 = (f32[2,2,256]{2,1,0:T(2,128)S(1)}, bf16[2,2,256,2048]{2,3,1,0:T(8,128)(2,1)}) fusion(bf16[256,2,2,128]{3,0,2,1:T(8,128)(2,1)S(1)} %get-tuple-element.405, bf16[4,2048,2,128]{3,1,0,2:T(8,128)(2,1)} %get-tuple-element.404, s32[]{:T(128)} %get-tuple-element.390, pred[256,2048]{0,1:T(8,128)(4,1)S(1)} %dynamic-slice_bitcast_fusion.5), kind=kOutput, calls=%fused_computation.14.clone.1 | convolution fusion | flops 549452800 | bytes 6033920 | tf_op jit(solution)/shard_map/while/body/eval_jaxpr/tkgd,skd->kgts/dot_general | solution.py:39
  199.4 3.4 fusion.47
  202.8 1.2 dynamic-slice_bitcast_fusion.5
  204.1 5.7 %convert_reduce_fusion.5 = (f32[2,2,256]{2,1,0:T(2,128)S(1)}, bf16[2,2,256,2048]{2,3,1,0:T(8,128)(2,1)}) fusion(bf16[256,2,2,128]{3,0,2,1:T(8,128)(2,1)S(1)} %get-tuple-element.405, bf16[4,2048,2,128]{3,1,0,2:T(8,128)(2,1)} %get-tuple-element.404, s32[]{:T(128)} %get-tuple-element.390, pred[256,2048]{0,1:T(8,128)(4,1)S(1)} %dynamic-slice_bitcast_fusion.5), kind=kOutput, calls=%fused_computation.14.clone.1 | convolution fusion | flops 549452800 | bytes 6033920 | tf_op jit(solution)/shard_map/while/body/eval_jaxpr/tkgd,skd->kgts/dot_general | solution.py:39
  209.7 3.5 fusion.47
  213.3 1.2 dynamic-slice_bitcast_fusion.5
  214.5 5.7 %convert_reduce_fusion.5 = (f32[2,2,256]{2,1,0:T(2,128)S(1)}, bf16[2,2,256,2048]{2,3,1,0:T(8,128)(2,1)}) fusion(bf16[256,2,2,128]{3,0,2,1:T(8,128)(2,1)S(1)} %get-tuple-element.405, bf16[4,2048,2,128]{3,1,0,2:T(8,128)(2,1)} %get-tuple-element.404, s32[]{:T(128)} %get-tuple-element.390, pred[256,2048]{0,1:T(8,128)(4,1)S(1)} %dynamic-slice_bitcast_fusion.5), kind=kOutput, calls=%fused_computation.14.clone.1 | convolution fusion | flops 549452800 | bytes 6033920 | tf_op jit(solution)/shard_map/while/body/eval_jaxpr/tkgd,skd->kgts/dot_general | solution.py:39
  220.2 3.5 fusion.47
  223.7 1.2 dynamic-slice_bitcast_fusion.5
  225.0 5.7 %convert_reduce_fusion.5 = (f32[2,2,256]{2,1,0:T(2,128)S(1)}, bf16[2,2,256,2048]{2,3,1,0:T(8,128)(2,1)}) fusion(bf16[256,2,2,128]{3,0,2,1:T(8,128)(2,1)S(1)} %get-tuple-element.405, bf16[4,2048,2,128]{3,1,0,2:T(8,128)(2,1)} %get-tuple-element.404, s32[]{:T(128)} %get-tuple-element.390, pred[256,2048]{0,1:T(8,128)(4,1)S(1)} %dynamic-slice_bitcast_fusion.5), kind=kOutput, calls=%fused_computation.14.clone.1 | convolution fusion | flops 549452800 | bytes 6033920 | tf_op jit(solution)/shard_map/while/body/eval_jaxpr/tkgd,skd->kgts/dot_general | solution.py:39
  230.6 3.4 fusion.47
  234.1 26.7 %all-gather.8.cloned.1.call-done = bf16[2,4096,2,128]{3,1,0,2:T(8,128)(2,1)} async-done(((bf16[2,128,2,128]{3,1,0,2:T(8,128)(2,1)}), bf16[2,4096,2,128]{3,1,0,2:T(8,128)(2,1)}) %all-gather.8.cloned.1.call-update) | async-done | bytes 4194320 | tf_op jit(solution)/shard_map/all_gather | solution.py:108
  260.8 26.7 %while.29 = (s32[]{:T(128)}, f32[256,2,2,128]{0,3,2,1:T(8,128)S(1)}, f32[2,2,256]{2,1,0:T(2,128)S(1)}, bf16[4,2048,2,128]{3,1,0,2:T(8,128)(2,1)}, pred[4,256,204...) while((s32[]{:T(128)}, ...), condition=%wide.region_8.9_spmd, body=%wide.region_6.8_spmd.sunk | while | flops 1086455808 | bytes 13386841 | solution.py:55
  260.8 0.2 dynamic-slice_bitcast_fusion.4
  261.0 4.3 %convert_reduce_fusion.4 = (f32[2,2,256]{2,1,0:T(2,128)S(1)}, bf16[2,2,256,2048]{2,3,1,0:T(8,128)(2,1)S(1)}) fusion(bf16[256,2,2,128]{3,0,2,1:T(8,128)(2,1)S(1)} %get-tuple-element.430, bf16[4,2048,2,128]{3,1,0,2:T(8,128)(2,1)} %get-tuple-element.429, s32[]{:T(128)} %get-tuple-element.416, pred[256,2048]{0,1:T(8,128)(4,1)S(1)} %dynamic-slice_bitcast_fusion.4), kind=kOutput, calls=%fused_computation.2.clone.1 | convolution fusion | flops 549452800 | bytes 6033920 | tf_op jit(solution)/shard_map/while/body/eval_jaxpr/tkgd,skd->kgts/dot_general | solution.py:39
  265.3 2.1 fusion.43
  267.5 0.2 dynamic-slice_bitcast_fusion.4
  267.6 4.3 %convert_reduce_fusion.4 = (f32[2,2,256]{2,1,0:T(2,128)S(1)}, bf16[2,2,256,2048]{2,3,1,0:T(8,128)(2,1)S(1)}) fusion(bf16[256,2,2,128]{3,0,2,1:T(8,128)(2,1)S(1)} %get-tuple-element.430, bf16[4,2048,2,128]{3,1,0,2:T(8,128)(2,1)} %get-tuple-element.429, s32[]{:T(128)} %get-tuple-element.416, pred[256,2048]{0,1:T(8,128)(4,1)S(1)} %dynamic-slice_bitcast_fusion.4), kind=kOutput, calls=%fused_computation.2.clone.1 | convolution fusion | flops 549452800 | bytes 6033920 | tf_op jit(solution)/shard_map/while/body/eval_jaxpr/tkgd,skd->kgts/dot_general | solution.py:39
  272.0 2.1 fusion.43
  274.1 0.2 dynamic-slice_bitcast_fusion.4
  274.3 4.3 %convert_reduce_fusion.4 = (f32[2,2,256]{2,1,0:T(2,128)S(1)}, bf16[2,2,256,2048]{2,3,1,0:T(8,128)(2,1)S(1)}) fusion(bf16[256,2,2,128]{3,0,2,1:T(8,128)(2,1)S(1)} %get-tuple-element.430, bf16[4,2048,2,128]{3,1,0,2:T(8,128)(2,1)} %get-tuple-element.429, s32[]{:T(128)} %get-tuple-element.416, pred[256,2048]{0,1:T(8,128)(4,1)S(1)} %dynamic-slice_bitcast_fusion.4), kind=kOutput, calls=%fused_computation.2.clone.1 | convolution fusion | flops 549452800 | bytes 6033920 | tf_op jit(solution)/shard_map/while/body/eval_jaxpr/tkgd,skd->kgts/dot_general | solution.py:39
  278.6 2.1 fusion.43
  280.8 0.2 dynamic-slice_bitcast_fusion.4
  281.0 4.3 %convert_reduce_fusion.4 = (f32[2,2,256]{2,1,0:T(2,128)S(1)}, bf16[2,2,256,2048]{2,3,1,0:T(8,128)(2,1)S(1)}) fusion(bf16[256,2,2,128]{3,0,2,1:T(8,128)(2,1)S(1)} %get-tuple-element.430, bf16[4,2048,2,128]{3,1,0,2:T(8,128)(2,1)} %get-tuple-element.429, s32[]{:T(128)} %get-tuple-element.416, pred[256,2048]{0,1:T(8,128)(4,1)S(1)} %dynamic-slice_bitcast_fusion.4), kind=kOutput, calls=%fused_computation.2.clone.1 | convolution fusion | flops 549452800 | bytes 6033920 | tf_op jit(solution)/shard_map/while/body/eval_jaxpr/tkgd,skd->kgts/dot_general | solution.py:39
  285.3 2.1 fusion.43
  287.6 0.2 copy.56
  287.7 0.1 reshape.214
  287.9 0.0 copy-start
  287.9 0.0 copy-start.3
  287.9 5.2 %convolution_convert_fusion = bf16[256,4608]{1,0:T(8,128)(2,1)} fusion(bf16[256,512]{1,0:T(8,128)(2,1)S(1)} %bitcast.117, bf16[512,4608]{1,0:T(8,128)(2,1)} %bitcast.118), kind=kOutput, calls=%fused_computation.27 | convolution fusion | flops 1209139200 | bytes 7340032 | tf_op jit(solution)/shard_map/dot_general | solution.py:137
  293.1 0.0 reduce-scatter.2.cloned.1.call-update
  293.1 81.8 %reduce-scatter.2.cloned.1.call-done = bf16[32,4608]{1,0:T(8,128)(2,1)} async-done(((bf16[256,4608]{1,0:T(8,128)(2,1)}), bf16[32,4608]{1,0:T(8,128)(2,1)}) %reduce-scatter.2.cloned.1.call-update) | async-done | bytes 294928 | tf_op jit(solution)/shard_map/reduce_scatter | solution.py:136
  375.0 1.1 multiply_reduce_fusion
  376.1 0.1 rsqrt.12
  376.2 1.8 add_convert_fusion
  (32 shorter events, 0.3 us)
Async XLA Ops:
  6.5 133.7 %all-gather.6.cloned.1.call-start = ((), (), s32[]{:S(2)}) async-start(), calls=%async_computation.3 | async-start | bytes 4325376 | tf_op jit(solution)/shard_map/all_gather | solution.py:89
  8.1 184.3 %all-gather.4.cloned.1.call-start = ((), (), s32[]{:S(2)}) async-start(), calls=%async_computation.2 | async-start | bytes 4325376 | tf_op jit(solution)/shard_map/all_gather | solution.py:90
  13.7 9.9 %copy-start.2 = (bf16[2,128,2,128]{3,2,1,0:T(2,128)(2,1)S(1)}, bf16[2,128,2,128]{3,2,1,0:T(2,128)(2,1)}, u32[]{:S(2)}) copy-start(bf16[2,128,2,128]{3,2,1,0:T(2,128)(2,1)} %param.15) | copy-start | bytes 393220
  13.7 10.7 %copy-start.4 = (s32[2,32]{1,0:T(2,128)S(1)}, s32[2,32]{1,0:T(2,128)}, u32[]{:S(2)}) copy-start(s32[2,32]{1,0:T(2,128)} %param.19) | copy-start | bytes 772
  13.7 11.1 %copy-start.5 = (s32[2]{0:T(128)S(1)}, s32[2]{0:T(128)}, u32[]{:S(2)}) copy-start(s32[2]{0:T(128)} %param.20) | copy-start | bytes 28
  13.7 121.7 %all-to-all-start = ((bf16[32,2,128,2,128]{4,2,1,3,0:T(8,128)(2,1)}), bf16[32,2,128,2,128]{4,2,1,3,0:T(8,128)(2,1)}, u32[]{:S(2)}, u32[]{:S(2)}) async-start(bf16[32,2,128,2,128]{4,2,1,3,0:T(8,128)(2,1)} %stack.2), calls=%async_computation | async-start | bytes 8388608 | tf_op jit(solution)/shard_map/all_to_all | solution.py:13
  23.6 9.8 %copy-start.1 = (bf16[2,128,4,128]{3,2,1,0:T(4,128)(2,1)S(1)}, bf16[2,128,4,128]{3,2,1,0:T(4,128)(2,1)}, u32[]{:S(2)}) copy-start(bf16[2,128,4,128]{3,2,1,0:T(4,128)(2,1)} %param.14) | copy-start | bytes 786436
  23.6 237.2 %all-gather.8.cloned.1.call-start = ((), (), s32[]{:S(2)}) async-start(), calls=%async_computation.4 | async-start | bytes 4325376 | tf_op jit(solution)/shard_map/all_gather | solution.py:108
  24.3 350.6 %reduce-scatter.2.cloned.1.call-start = ((), (), s32[]{:S(2)}) async-start(), calls=%async_computation.5 | async-start | bytes 2654208 | tf_op jit(solution)/shard_map/reduce_scatter | solution.py:136
  287.9 88.3 %copy-start = (bf16[2,16,4608]{2,1,0:T(8,128)(2,1)S(1)}, bf16[2,16,4608]{2,1,0:T(8,128)(2,1)}, u32[]{:S(2)}) copy-start(bf16[2,16,4608]{2,1,0:T(8,128)(2,1)} %param.22) | copy-start | bytes 884740
  287.9 88.3 %copy-start.3 = (f32[4608]{0:T(1024)S(1)}, f32[4608]{0:T(1024)}, u32[]{:S(2)}) copy-start(f32[4608]{0:T(1024)} %param.23) | copy-start | bytes 55300
Sparse Core Ops, SparseCore 0:
  9.2 109.6 all-gather.5
  120.8 71.6 all-gather.3
  194.3 66.3 all-gather.7
  293.2 81.6 reduce-scatter.1
